TPU v7x, 32 devices: a whole 2x2x4 slice. The times are simulated.
32 devices in a mesh: row: 16 (over z, y, core), col: 2 (over x).
Axes of the slice: x: 2, y: 2, z: 4, core: 2. Of those that a mesh axis runs over, the one named last changes fastest.
Arguments:
- seq: float32 [768, 1024], P('row', 'col'), may hold values from -6 to 6
- query: float32 [768, 1024], P('row', 'col'), may hold values from -24 to 24, as said below
- key: float32 [768, 1024], P('col', 'row'), may hold values from -24 to 24, as said below
- value: float32 [768, 1024], P('col', 'row'), may hold values from -6 to 6
- pair: float32 [768, 768, 128], P('row', 'col'), may hold values from -6 to 6
- w_bias: float32 [128, 32], replicated, may hold values from -0.5 to 0.5
- w_out: float32 [1024, 1024], P(None, 'col'), may hold values from -0.75 to 0.75
- w_left: float32 [1024, 64], P('col'), may hold values from -0.1875 to 0.1875
- w_right: float32 [1024, 64], P('col'), may hold values from -0.1875 to 0.1875
- w_outer: float32 [128, 128], replicated, may hold values from -0.5 to 0.5
- outer_bias: float32 [128], replicated, may hold values from -3 to 3
- w_up: float32 [128, 512], replicated, may hold values from -0.5 to 0.5
- w_down: float32 [512, 128], replicated, may hold values from -0.25 to 0.25
Outputs:
- seq_new: float32 [768, 1024], P('row', 'col')
- pair_new: float32 [768, 768, 128], P('row', 'col')
Inputs may be any that keep to these rules, and one draw needn't show every extreme that they name: `query`: Head-major queries of order one; some residues may be much larger. `key`: Head-major keys of order one; some residues may be much larger.
All inputs are finite; a program needn't handle non-finite values.
Results may differ from a plain program's by a relative error of at most 0.0003.
Values sent between devices are 32-bit elements; how exact they have to be, the bound alone decides.
A program may use at most 128 MiB of HBM per device.

v0:
```python
import jax
import jax.numpy as jnp
from jax import lax
from jax.sharding import PartitionSpec as P

HIGH = lax.Precision.HIGHEST


def merged(x, axis, combine):
    everything = jax.tree.map(lambda part: lax.all_gather(part, axis), x)
    leading = jax.tree.map(lambda part: part[0], everything)

    def hop(k, so_far):
        return combine(so_far, jax.tree.map(lambda part: part[k], everything))

    return lax.fori_loop(1, lax.axis_size(axis), hop, leading)


def channel_norm(x):
    centre = x - jnp.mean(x, axis=-1, keepdims=True)
    return centre * lax.rsqrt(jnp.mean(centre * centre, axis=-1, keepdims=True) + 1e-05)


def combine(first, second):
    top = jnp.maximum(first[0], second[0])
    scale_one = jnp.exp(first[0] - top)
    scale_two = jnp.exp(second[0] - top)
    totals = first[1] * scale_one + second[1] * scale_two
    weighted = first[2] * scale_one[..., None] + second[2] * scale_two[..., None]
    return (top, totals, weighted)


def partial_softmax(q_heads, k_heads, v_heads, bias, scale):
    scores = jnp.einsum("ihd,jhd->ihj", q_heads, k_heads, precision=HIGH) * scale + bias
    top = jnp.max(scores, axis=2)
    expo = jnp.exp(scores - top[..., None])
    totals = jnp.sum(expo, axis=2)
    weighted = jnp.einsum("ihj,jhd->ihd", expo, v_heads, precision=HIGH)
    return (top, totals, weighted)


def per_device(
    seq, query, key, value, pair, w_bias, w_out, w_left, w_right, w_outer, outer_bias, w_up, w_down
):
    rows_here = pair.shape[0]
    cols_here = pair.shape[1]
    channels = pair.shape[2]
    heads = w_bias.shape[1]
    width = w_out.shape[0]
    head_dim = width // heads
    proj_width = w_left.shape[1]
    scale = 1.0 / jnp.sqrt(jnp.float32(head_dim))
    bias = jnp.einsum("ijc,ch->ihj", channel_norm(pair), w_bias, precision=HIGH)
    queries = lax.all_gather(query, "col", axis=1, tiled=True)
    keys_all, values_all = (
        lax.all_gather(key, "row", axis=1, tiled=True),
        lax.all_gather(value, "row", axis=1, tiled=True),
    )
    parts = partial_softmax(
        queries.reshape(rows_here, heads, head_dim),
        keys_all.reshape(cols_here, heads, head_dim),
        values_all.reshape(cols_here, heads, head_dim),
        bias,
        scale,
    )
    top, totals, weighted = merged(parts, "col", combine)
    attn = (weighted / totals[..., None]).reshape(rows_here, width)
    seq_new = seq + jnp.dot(attn, w_out, precision=HIGH)
    sum_value, sum_square = lax.psum(
        (jnp.sum(seq_new, axis=1), jnp.sum(seq_new * seq_new, axis=1)), "col"
    )
    mean_value = (sum_value / width)[:, None]
    mean_square = (sum_square / width)[:, None]
    seq_norm = (seq_new - mean_value) * lax.rsqrt(mean_square - mean_value * mean_value + 1e-05)
    left_part = jnp.dot(seq_norm, w_left, precision=HIGH)
    right_part = jnp.dot(seq_norm, w_right, precision=HIGH)
    left, right = lax.psum((left_part, right_part), "col")
    right_every = lax.all_gather(right, "row", axis=0, tiled=True)
    start = lax.axis_index("col") * cols_here
    right_block = lax.dynamic_slice_in_dim(right_every, start, cols_here, 0)
    w_prod = w_outer[:proj_width]
    w_diff = w_outer[proj_width:]
    table = right_block[:, :, None] * w_prod[None, :, :]
    left_diff = jnp.dot(left, w_diff, precision=HIGH)
    right_diff = jnp.dot(right_block, w_diff, precision=HIGH)
    outer = (
        jnp.einsum("ip,jpc->ijc", left, table, precision=HIGH)
        + left_diff[:, None, :]
        - right_diff[None, :, :]
        + outer_bias
    )
    pair_mid = pair + outer
    flat = pair_mid.reshape(rows_here * cols_here, channels)
    hidden_act = jax.nn.relu(jnp.dot(channel_norm(flat), w_up, precision=HIGH))
    pair_new = flat + jnp.dot(hidden_act, w_down, precision=HIGH)
    return (seq_new, pair_new.reshape(rows_here, cols_here, channels))


def solution(mesh):
    in_specs = (
        P("row", "col"),
        P("row", "col"),
        P("col", "row"),
        P("col", "row"),
        P("row", "col", None),
        P(),
        P(None, "col"),
        P("col", None),
        P("col", None),
        P(),
        P(),
        P(),
        P(),
    )
    out_specs = (P("row", "col"), P("row", "col", None))
    return jax.shard_map(
        per_device, mesh=mesh, in_specs=in_specs, out_specs=out_specs, check_vma=False
    )
```

profile of v0, /device:TPU:0, one launch (start us, length us, event | category | flops | bytes accessed | tf_op | source)
XLA Modules:
  0.0 295.0 jit_solution(9783816739350070599)
XLA Ops:
  7.2 0.7 all-gather.8.cloned.1.call-update
  8.0 0.7 all-gather.10.cloned.1.call-update
  8.7 6.7 %all_gather.31 = f32[48,1024]{1,0:T(8,128)S(1)} all-gather(f32[48,512]{1,0:T(8,128)} %param.14), channel_id=1, replica_groups=mesh['row'=16,'col'=2] {'col'}, dimensions={1}, use_global_device_ids=true | all-gather | bytes 294912 | tf_op jit(solution)/shard_map/all_gather | solution.py:54
  15.6 6.2 %reduce_sum.63 = f32[48,384]{1,0:T(8,128)S(1)} reduce(f32[48,384,128]{2,1,0:T(8,128)} %param.17, f32[]{:T(128)} %constant.13.clone.1), dimensions={2}, to_apply=%region_0.0 | reduce | flops 2340864 | bytes 9510916 | tf_op jit(solution)/shard_map/reduce_sum | solution.py:20
  21.8 7.7 %multiply_reduce_fusion.1 = f32[48,384]{1,0:T(8,128)S(1)} fusion(f32[48,384,128]{2,1,0:T(8,128)} %param.17, f32[48,384]{1,0:T(8,128)S(1)} %broadcast_multiply_fusion.1), kind=kLoop, calls=%fused_computation.12 | loop fusion | flops 7059456 | bytes 9584640 | tf_op jit(solution)/shard_map/reduce_sum | solution.py:21
  29.5 15.9 %fusion.9 = f32[48,384,32]{1,2,0:T(8,128)} fusion(f32[48,384,128]{2,1,0:T(8,128)} %param.17, f32[48,384]{1,0:T(8,128)S(1)} %add_rsqrt_fusion.1, f32[48,384]{1,0:T(8,128)S(1)} %broadcast_multiply_fusion.1, f32[128,32]{0,1:T(8,128)S(1)} %copy-done.7), kind=kOutput, calls=%fused_computation.10 | convolution fusion | flops 910688256 | bytes 11960320 | tf_op jit(solution)/shard_map/ijc,ch->ihj/dot_general | solution.py:53
  45.4 7.2 %all-gather.8.cloned.1.call-done = f32[384,1024]{0,1:T(8,128)} async-done(((f32[384,64]{0,1:T(8,128)}), f32[384,1024]{0,1:T(8,128)}) %all-gather.8.cloned.1.call-update) | async-done | bytes 1572880 | tf_op jit(solution)/shard_map/all_gather | solution.py:56
  52.6 5.7 %fusion.45 = (f32[48,32]{0,1:T(8,128)S(1)}, f32[48,32,384]{2,0,1:T(8,128)S(1)}) fusion(f32[48,384,32]{1,2,0:T(8,128)} %fusion.9, f32[384,32,32]{0,2,1:T(8,128)} %bitcast.72, f32[48,32,32]{0,2,1:T(8,128)S(1)} %bitcast.70), kind=kOutput, calls=%fused_computation.63 | convolution fusion | flops 228260352 | bytes 6494208 | tf_op jit(solution)/shard_map/ihd,jhd->ihj/dot_general | solution.py:34
  58.3 1.4 copy-done.2
  59.7 0.8 fusion.18
  60.5 32.7 %all-gather.10.cloned.1.call-done = f32[384,1024]{0,1:T(8,128)} async-done(((f32[384,64]{0,1:T(8,128)}), f32[384,1024]{0,1:T(8,128)}) %all-gather.10.cloned.1.call-update) | async-done | bytes 1572880 | tf_op jit(solution)/shard_map/all_gather | solution.py:57
  93.3 5.1 %fusion.20 = f32[48,32,32]{0,2,1:T(8,128)S(1)} fusion(f32[384,32,32]{0,2,1:T(8,128)} %bitcast.71, f32[48,32,384]{2,0,1:T(8,128)} %copy-done.2, f32[48,32]{0,1:T(8,128)S(1)} %get-tuple-element.37), kind=kOutput, calls=%fused_computation.22 | convolution fusion | flops 227082240 | bytes 4134912 | tf_op jit(solution)/shard_map/ihj,jhd->ihd/dot_general | solution.py:38
  98.3 4.4 %all-gather.3 = f32[2,48,32]{1,2,0:T(8,128)S(1)} all-gather(f32[1,48,32]{1,2,0:T(8,128)S(1)} %bitcast.73), channel_id=3, replica_groups=mesh['row'=16,'col'=2] {'col'}, dimensions={0}, use_global_device_ids=true | all-gather | bytes 18432 | tf_op jit(solution)/shard_map/all_gather | solution.py:10
  102.8 4.4 %all-gather.4 = f32[2,48,32]{1,2,0:T(8,128)S(1)} all-gather(f32[1,48,32]{1,2,0:T(8,128)S(1)} %bitcast.74), channel_id=4, replica_groups=mesh['row'=16,'col'=2] {'col'}, dimensions={0}, use_global_device_ids=true | all-gather | bytes 18432 | tf_op jit(solution)/shard_map/all_gather | solution.py:10
  107.3 0.7 copy.53
  108.0 0.7 copy.51
  108.7 18.0 %all-gather = f32[96,32,32]{2,1,0:T(8,128)S(1)} all-gather(f32[48,32,32]{2,1,0:T(8,128)S(1)} %copy.51), channel_id=2, replica_groups=mesh['row'=16,'col'=2] {'col'}, dimensions={0}, use_global_device_ids=true | all-gather | bytes 589824 | tf_op jit(solution)/shard_map/all_gather | solution.py:10
  126.8 2.0 fusion.23
  128.8 0.4 reshape.150
  129.2 2.3 fusion.42
  131.5 4.9 %all-reduce.1 = (f32[48]{0:T(128)S(1)}, f32[48]{0:T(128)S(1)}) all-reduce(f32[48]{0:T(128)S(1)} %get-tuple-element.19, f32[48]{0:T(128)S(1)} %get-tuple-element.18), channel_id=1, replica_groups=mesh['row'=16,'col'=2] {'col'}, use_global_device_ids=true, to_apply=%region_7.0 | all-reduce | flops 96 | bytes 768 | tf_op jit(solution)/shard_map/psum | solution.py:69
  136.5 1.2 fusion.24
  137.7 1.2 fusion.25
  138.9 8.6 %all-reduce = (f32[48,64]{1,0:T(8,128)S(1)}, f32[48,64]{1,0:T(8,128)S(1)}) all-reduce(f32[48,64]{1,0:T(8,128)S(1)} %fusion.24, f32[48,64]{1,0:T(8,128)S(1)} %fusion.25), channel_id=1, replica_groups=mesh['row'=16,'col'=2] {'col'}, use_global_device_ids=true, to_apply=%region_9.0 | all-reduce | flops 6144 | bytes 49152 | tf_op jit(solution)/shard_map/psum | solution.py:77
  147.6 20.2 %all_gather.39 = f32[768,64]{1,0:T(8,128)S(1)} all-gather(f32[48,64]{1,0:T(8,128)S(1)} %get-tuple-element.20), channel_id=1, replica_groups=mesh['row'=16,'col'=2] {'row'}, dimensions={0}, use_global_device_ids=true | all-gather | bytes 208896 | tf_op jit(solution)/shard_map/all_gather | solution.py:78
  167.9 0.3 fusion.30
  168.2 22.6 %fusion.46 = (f32[48,384]{0,1:T(8,128)S(1)}, f32[48,384,128]{2,0,1:T(8,128)}) fusion(f32[128]{0:T(128)S(1)} %copy-done.8, f32[384,128]{1,0:T(8,128)S(1)} %fusion.30, f32[48,128]{1,0:T(8,128)S(1)} %fusion.32, f32[64,128]{1,0:T(8,128)S(1)} %slice-done.6, f32[384,64]{1,0:T(8,128)S(1)} %constant_dynamic-slice_fusion, f32[48,64]{1,0:T(8,128)S(1)} %get-tuple-element.21, ...), kind=kOutput, calls=%fused_computation.64 | convolution fusion | flops 1826863104 | bytes 19313152 | tf_op jit(solution)/shard_map/ip,jpc->ijc/dot_general | solution.py:87
  191.1 10.5 %copy.56 = f32[48,384,128]{2,1,0:T(8,128)} copy(f32[48,384,128]{2,0,1:T(8,128)} %get-tuple-element.41) | data formatting | bytes 18874368 | tf_op jit(solution)/shard_map/add | solution.py:92
  201.6 5.4 %multiply_reduce_fusion = f32[48,384]{0,1:T(8,128)S(1)} fusion(f32[48,384,128]{2,0,1:T(8,128)S(1)} %bitcast.65, f32[48,384]{0,1:T(8,128)S(1)} %copy.58), kind=kLoop, calls=%fused_computation.9 | loop fusion | flops 7059456 | bytes 9584640 | tf_op jit(solution)/shard_map/reduce_sum | solution.py:21
  207.2 11.4 %fusion.8 = f32[18432,128]{1,0:T(8,128)S(1)} fusion(f32[48,384,128]{2,1,0:T(8,128)} %copy.56, f32[18432]{0:T(1024)S(1)} %rsqrt.26, f32[18432]{0:T(1024)S(1)} %div.39), kind=kLoop, calls=%fused_computation.7 | loop fusion | flops 4718592 | bytes 19021824 | tf_op jit(solution)/shard_map/mul | solution.py:21
  218.6 33.8 %fusion.47 = f32[18432,512]{1,0:T(8,128)} fusion(f32[18432,128]{1,0:T(8,128)S(1)} %fusion.8, f32[128,512]{1,0:T(8,128)S(1)} %copy-done.5), kind=kOutput, calls=%fused_computation.65 | convolution fusion | flops 14495514624 | bytes 47448064 | tf_op jit(solution)/shard_map/dot_general | solution.py:94
  252.4 35.4 %fusion.2 = f32[18432,128]{1,0:T(8,128)} fusion(f32[18432,128]{1,0:T(8,128)S(1)} %bitcast.68, f32[512,128]{1,0:T(8,128)S(1)} %copy-done.6, f32[18432,512]{1,0:T(8,128)} %fusion.47), kind=kOutput, calls=%fused_computation.2 | convolution fusion | flops 14507311104 | bytes 56885248 | tf_op jit(solution)/shard_map/dot_general | solution.py:95
  (51 shorter events, 1.1 us)
Async XLA Ops:
  7.2 122.0 %copy-start = (f32[1024,512]{1,0:T(8,128)S(1)}, f32[1024,512]{1,0:T(8,128)}, u32[]{:S(2)}) copy-start(f32[1024,512]{1,0:T(8,128)} %param.19) | copy-start | bytes 6291460
  7.2 45.5 %all-gather.8.cloned.1.call-start = ((), (), s32[]{:S(2)}) async-start(), calls=%async_computation | async-start | bytes 1671168 | tf_op jit(solution)/shard_map/all_gather | solution.py:56
  7.9 85.3 %all-gather.10.cloned.1.call-start = ((), (), s32[]{:S(2)}) async-start(), calls=%async_computation.1 | async-start | bytes 1671168 | tf_op jit(solution)/shard_map/all_gather | solution.py:57
  15.6 14.0 %copy-start.7 = (f32[128,32]{0,1:T(8,128)S(1)}, f32[128,32]{0,1:T(8,128)}, u32[]{:S(2)}) copy-start(f32[128,32]{0,1:T(8,128)} %param.18) | copy-start | bytes 49156
  58.3 1.4 copy-start.2
  58.3 89.2 %copy-start.4 = (f32[128,128]{1,0:T(8,128)S(1)}, f32[128,128]{1,0:T(8,128)}, u32[]{:S(2)}) copy-start(f32[128,128]{1,0:T(8,128)} %param.22) | copy-start | bytes 196612
  58.3 109.8 %slice-start.6 = ((f32[128,128]{1,0:T(8,128)}), f32[64,128]{1,0:T(8,128)S(1)}, s32[]{:S(2)}) async-start(f32[128,128]{1,0:T(8,128)} %param.22), calls=%async_computation.8 | async-start | bytes 65536 | tf_op jit(solution)/shard_map/slice | solution.py:81
  108.7 59.4 %copy-start.8 = (f32[128]{0:T(128)S(1)}, f32[128]{0:T(128)}, u32[]{:S(2)}) copy-start(f32[128]{0:T(128)} %param.23) | copy-start | bytes 1540
  131.5 59.3 %copy-start.3 = (f32[48,512]{1,0:T(8,128)}, f32[48,512]{1,0:T(8,128)S(1)}, u32[]{:S(2)}) copy-start(f32[48,512]{1,0:T(8,128)S(1)} %get-tuple-element.39) | copy-start | bytes 294916
  190.9 10.6 %slice-start = ((s8[9437184]{0:T(1024)(128)(4,1)}), s8[1048576]{0:T(1024)(128)(4,1)S(1)}, s32[]{:S(2)}) async-start(s8[9437184]{0:T(1024)(128)(4,1)} %bitcast.64), calls=%async_computation.2 | async-start | bytes 2097152
  191.1 10.5 %slice-start.1 = ((s8[9437184]{0:T(1024)(128)(4,1)}), s8[4194304]{0:T(1024)(128)(4,1)S(1)}, s32[]{:S(2)}) async-start(s8[9437184]{0:T(1024)(128)(4,1)} %bitcast.64), calls=%async_computation.3 | async-start | bytes 8388608
  191.1 10.5 %slice-start.2 = ((s8[9437184]{0:T(1024)(128)(4,1)}), s8[4194304]{0:T(1024)(128)(4,1)S(1)}, s32[]{:S(2)}) async-start(s8[9437184]{0:T(1024)(128)(4,1)} %bitcast.64), calls=%async_computation.4 | async-start | bytes 8388608
  207.1 11.4 %copy-start.5 = (f32[128,512]{1,0:T(8,128)S(1)}, f32[128,512]{1,0:T(8,128)}, u32[]{:S(2)}) copy-start(f32[128,512]{1,0:T(8,128)} %param.24) | copy-start | bytes 786436
  207.2 45.3 %slice-start.3 = ((s8[9437184]{0:T(1024)(128)(4,1)}), s8[4194304]{0:T(1024)(128)(4,1)S(1)}, s32[]{:S(2)}) async-start(s8[9437184]{0:T(1024)(128)(4,1)} %bitcast.66), calls=%async_computation.5 | async-start | bytes 8388608
  218.6 33.8 %slice-start.4 = ((s8[9437184]{0:T(1024)(128)(4,1)}), s8[4194304]{0:T(1024)(128)(4,1)S(1)}, s32[]{:S(2)}) async-start(s8[9437184]{0:T(1024)(128)(4,1)} %bitcast.66), calls=%async_computation.6 | async-start | bytes 8388608
  218.6 33.8 %slice-start.5 = ((s8[9437184]{0:T(1024)(128)(4,1)}), s8[1048576]{0:T(1024)(128)(4,1)S(1)}, s32[]{:S(2)}) async-start(s8[9437184]{0:T(1024)(128)(4,1)} %bitcast.66), calls=%async_computation.7 | async-start | bytes 2097152
  218.6 33.8 %copy-start.6 = (f32[512,128]{1,0:T(8,128)S(1)}, f32[512,128]{1,0:T(8,128)}, u32[]{:S(2)}) copy-start(f32[512,128]{1,0:T(8,128)} %param.25) | copy-start | bytes 786436
  252.4 35.5 %copy-start.1 = (f32[1024,512]{1,0:T(8,128)S(1)}, f32[1024,512]{1,0:T(8,128)}, u32[]{:S(2)}) copy-start(f32[1024,512]{1,0:T(8,128)} %param.19) | copy-start | bytes 6291460
Sparse Core Ops, SparseCore 0:
  10.3 42.3 all-gather.7
  54.9 38.2 all-gather.9
where the time goes:
time: 298 us; the launch traced here: 295 us
  matrix products  124 us (42%)
  blocking collectives  67.2 us (23%)
  waiting for transfers between devices  41.3 us (14%)
  other arithmetic  33.6 us (11%)
  between operations  14.6 us (5%)
  local copies, waits for them, and re-layouts  14.4 us (5%)
    dot_general x1, matrix products, per_device(): pair_new = flat + jnp.dot(hidden_act, w_down, precision=HIGH)  35.4 us
    dot_general x1, matrix products, per_device(): hidden_act = jax.nn.relu(jnp.dot(channel_norm(flat), w_up, precision=HIGH))  33.8 us
    all_gather x1, waiting for transfers between devices, per_device(): lax.all_gather(value, 'row', axis=1, tiled=True)  32.7 us
    all_gather x3, blocking collectives, merged(): everything = jax.tree.map(lambda part: lax.all_gather(part, axis), x)  26.8 us
    dot_general x1, matrix products, per_device(): jnp.einsum('ip,jpc->ijc', left, table, precision=HIGH)  22.6 us
    all_gather x1, blocking collectives, per_device(): right_every = lax.all_gather(right, 'row', axis=0, tiled=True)  20.2 us
    dot_general x1, matrix products, per_device(): bias = jnp.einsum('ijc,ch->ihj', channel_norm(pair), w_bias, precision=HIGH)  15.9 us
    reduce_sum x2, other arithmetic, channel_norm(): jnp.mean(centre * centre, axis=-1, keepdims=True) + 1e-05  13.1 us
  transfers between devices with their start and end apart: 2, of which 2 were waited for; matrix products, arithmetic and copies ran while one was open for 12% of the time, Pallas kernels for 0%

commit v1 on v0

--- a/solution.py
+++ b/solution.py
@@ -2,8 +2,26 @@
 import jax.numpy as jnp
 from jax import lax
 from jax.sharding import PartitionSpec as P
+from jax.lax import axis_index, axis_size, ppermute
 
 HIGH = lax.Precision.HIGHEST
+
+
+def matrix_watch(shard_in):
+    group_axis = "row"
+    a_next = axis_size(group_axis)
+    step_out, current_block, w_next = (a_next, axis_index(group_axis), shard_in.shape[1])
+    vals = [b * step_out if d == 1 else b for d, b in enumerate(shard_in.shape)]
+    view_out = jnp.zeros(vals, shard_in.dtype)
+    n_now = lax.dynamic_update_slice_in_dim(view_out, shard_in, current_block * w_next, axis=1)
+    for it in range(1, step_out):
+        shard_in = ppermute(
+            shard_in, group_axis, list(map(lambda d: (d, (d + 1) % step_out), range(step_out)))
+        )
+        n_now = lax.dynamic_update_slice_in_dim(
+            n_now, shard_in, (current_block - it) % step_out * w_next, axis=1
+        )
+    return n_now
 
 
 def merged(x, axis, combine):
@@ -52,10 +70,7 @@
     scale = 1.0 / jnp.sqrt(jnp.float32(head_dim))
     bias = jnp.einsum("ijc,ch->ihj", channel_norm(pair), w_bias, precision=HIGH)
     queries = lax.all_gather(query, "col", axis=1, tiled=True)
-    keys_all, values_all = (
-        lax.all_gather(key, "row", axis=1, tiled=True),
-        lax.all_gather(value, "row", axis=1, tiled=True),
-    )
+    keys_all, values_all = (lax.all_gather(key, "row", axis=1, tiled=True), matrix_watch(value))
     parts = partial_softmax(
         queries.reshape(rows_here, heads, head_dim),
         keys_all.reshape(cols_here, heads, head_dim),

time: 298 us -> 346 us (1.16)
  waiting for transfers between devices: 41.3 us -> 85.4 us
  local copies, waits for them, and re-layouts: 14.4 us -> 24 us
  blocking collectives: 67.2 us -> 61.3 us
    ppermute x0 -> x15, waiting for transfers between devices: none -> 84.7 us  [matrix_watch(): ppermute(shard_in, group_axis, list(map(lambda d: (d, (d + 1) % step_out)...]
    all_gather x1 -> x0, waiting for transfers between devices: 32.7 us -> none  [per_device(): lax.all_gather(value, 'row', axis=1, tiled=True)]
    dynamic_update_slice x0 -> x16, local copies, waits for them, and re-layouts: none -> 10.3 us  [the longest x15 9.65 us: matrix_watch(): lax.dynamic_update_slice_in_dim(n_now, shard_in, (current_block - it) % s...]
    all_gather x1, waiting for transfers between devices: 7.2 us -> 0.01 us  [per_device(): lax.all_gather(key, 'row', axis=1, tiled=True)]
    all_gather x3, blocking collectives: 26.8 us -> 22.2 us  [merged(): everything = jax.tree.map(lambda part: lax.all_gather(part, axis), x)]
  transfers between devices with their start and end apart: 2 -> 16, of which waited for: 2 -> 14; matrix products, arithmetic and copies ran while one was open for 12% -> 12% of each run, Pallas kernels for 0% -> 0%
where the time goes in v1:
time: 346 us; the launch traced here: 340 us
  matrix products  121 us (35%)
  waiting for transfers between devices  85.4 us (25%)
  blocking collectives  61.3 us (18%)
  other arithmetic  32.1 us (9%)
  local copies, waits for them, and re-layouts  24 us (7%)
  between operations  14.8 us (4%)
    ppermute x15, waiting for transfers between devices, matrix_watch(): ppermute(shard_in, group_axis, list(map(lambda d: (d, (d + 1) % step_out)...  84.7 us
    dot_general x1, matrix products, per_device(): pair_new = flat + jnp.dot(hidden_act, w_down, precision=HIGH)  35.4 us
    dot_general x1, matrix products, per_device(): hidden_act = jax.nn.relu(jnp.dot(channel_norm(flat), w_up, precision=HIGH))  33.8 us
    dot_general x1, matrix products, per_device(): jnp.einsum('ip,jpc->ijc', left, table, precision=HIGH)  22.6 us
    all_gather x3, blocking collectives, merged(): everything = jax.tree.map(lambda part: lax.all_gather(part, axis), x)  22.2 us
    all_gather x1, blocking collectives, per_device(): right_every = lax.all_gather(right, 'row', axis=0, tiled=True)  18.8 us
    dot_general x1, matrix products, per_device(): bias = jnp.einsum('ijc,ch->ihj', channel_norm(pair), w_bias, precision=HIGH)  15.9 us
    reduce_sum x2, other arithmetic, channel_norm(): jnp.mean(centre * centre, axis=-1, keepdims=True) + 1e-05  12.9 us
  transfers between devices with their start and end apart: 16, of which 14 were waited for; matrix products, arithmetic and copies ran while one was open for 12% of the time, Pallas kernels for 0%

profile of v1, /device:TPU:0, one launch (start us, length us, event | category | flops | bytes accessed | tf_op | source)
XLA Modules:
  0.0 340.3 jit_solution(10046917571931203702)
XLA Ops:
  8.5 6.2 %reduce_sum.63 = f32[48,384]{1,0:T(8,128)S(1)} reduce(f32[48,384,128]{2,1,0:T(8,128)} %param.17, f32[]{:T(128)} %constant.133.clone.1), dimensions={2}, to_apply=%region_0.0 | reduce | flops 2340864 | bytes 9510916 | tf_op jit(solution)/shard_map/reduce_sum | solution.py:38
  14.7 6.4 %all_gather.28 = f32[48,1024]{1,0:T(8,128)S(1)} all-gather(f32[48,512]{1,0:T(8,128)S(1)} %copy-done.9), channel_id=1, replica_groups=mesh['row'=16,'col'=2] {'col'}, dimensions={1}, use_global_device_ids=true | all-gather | bytes 294912 | tf_op jit(solution)/shard_map/all_gather | solution.py:72
  21.4 7.4 %multiply_reduce_fusion.1 = f32[48,384]{1,0:T(8,128)S(1)} fusion(f32[48,384,128]{2,1,0:T(8,128)} %param.17, f32[48,384]{1,0:T(8,128)S(1)} %broadcast_multiply_fusion.1), kind=kLoop, calls=%fused_computation.12 | loop fusion | flops 7059456 | bytes 9584640 | tf_op jit(solution)/shard_map/reduce_sum | solution.py:39
  28.9 15.9 %fusion.9 = f32[48,384,32]{1,2,0:T(8,128)} fusion(f32[48,384,128]{2,1,0:T(8,128)} %param.17, f32[48,384]{1,0:T(8,128)S(1)} %add_rsqrt_fusion.1, f32[48,384]{1,0:T(8,128)S(1)} %broadcast_multiply_fusion.1, f32[128,32]{0,1:T(8,128)S(1)} %copy-done.10), kind=kOutput, calls=%fused_computation.10 | convolution fusion | flops 910688256 | bytes 11960320 | tf_op jit(solution)/shard_map/ijc,ch->ihj/dot_general | solution.py:71
  47.9 5.5 %collective-permute-done.1 = f32[384,64]{0,1:T(8,128)S(1)} collective-permute-done((f32[384,64]{0,1:T(8,128)S(1)}, f32[384,64]{0,1:T(8,128)S(1)}, u32[]{:S(2)}, u32[]{:S(2)}) %collective-permute-start.1) | collective-permute-done | bytes 98336 | tf_op jit(solution)/shard_map/ppermute | solution.py:18
  54.1 6.1 %collective-permute-done.2 = f32[384,64]{0,1:T(8,128)S(1)} collective-permute-done((f32[384,64]{0,1:T(8,128)S(1)}, f32[384,64]{0,1:T(8,128)S(1)}, u32[]{:S(2)}, u32[]{:S(2)}) %collective-permute-start.2) | collective-permute-done | bytes 98336 | tf_op jit(solution)/shard_map/ppermute | solution.py:18
  60.8 6.1 %collective-permute-done.3 = f32[384,64]{0,1:T(8,128)S(1)} collective-permute-done((f32[384,64]{0,1:T(8,128)S(1)}, f32[384,64]{0,1:T(8,128)S(1)}, u32[]{:S(2)}, u32[]{:S(2)}) %collective-permute-start.3) | collective-permute-done | bytes 98336 | tf_op jit(solution)/shard_map/ppermute | solution.py:18
  67.5 6.1 %collective-permute-done.4 = f32[384,64]{0,1:T(8,128)S(1)} collective-permute-done((f32[384,64]{0,1:T(8,128)S(1)}, f32[384,64]{0,1:T(8,128)S(1)}, u32[]{:S(2)}, u32[]{:S(2)}) %collective-permute-start.4) | collective-permute-done | bytes 98336 | tf_op jit(solution)/shard_map/ppermute | solution.py:18
  74.3 6.1 %collective-permute-done.5 = f32[384,64]{0,1:T(8,128)S(1)} collective-permute-done((f32[384,64]{0,1:T(8,128)S(1)}, f32[384,64]{0,1:T(8,128)S(1)}, u32[]{:S(2)}, u32[]{:S(2)}) %collective-permute-start.5) | collective-permute-done | bytes 98336 | tf_op jit(solution)/shard_map/ppermute | solution.py:18
  81.0 6.1 %collective-permute-done.6 = f32[384,64]{0,1:T(8,128)S(1)} collective-permute-done((f32[384,64]{0,1:T(8,128)S(1)}, f32[384,64]{0,1:T(8,128)S(1)}, u32[]{:S(2)}, u32[]{:S(2)}) %collective-permute-start.6) | collective-permute-done | bytes 98336 | tf_op jit(solution)/shard_map/ppermute | solution.py:18
  87.8 6.1 %collective-permute-done.7 = f32[384,64]{0,1:T(8,128)S(1)} collective-permute-done((f32[384,64]{0,1:T(8,128)S(1)}, f32[384,64]{0,1:T(8,128)S(1)}, u32[]{:S(2)}, u32[]{:S(2)}) %collective-permute-start.7) | collective-permute-done | bytes 98336 | tf_op jit(solution)/shard_map/ppermute | solution.py:18
  94.5 6.1 %collective-permute-done.8 = f32[384,64]{0,1:T(8,128)S(1)} collective-permute-done((f32[384,64]{0,1:T(8,128)S(1)}, f32[384,64]{0,1:T(8,128)S(1)}, u32[]{:S(2)}, u32[]{:S(2)}) %collective-permute-start.8) | collective-permute-done | bytes 98336 | tf_op jit(solution)/shard_map/ppermute | solution.py:18
  101.2 6.1 %collective-permute-done.9 = f32[384,64]{0,1:T(8,128)S(1)} collective-permute-done((f32[384,64]{0,1:T(8,128)S(1)}, f32[384,64]{0,1:T(8,128)S(1)}, u32[]{:S(2)}, u32[]{:S(2)}) %collective-permute-start.9) | collective-permute-done | bytes 98336 | tf_op jit(solution)/shard_map/ppermute | solution.py:18
  108.0 6.1 %collective-permute-done.10 = f32[384,64]{0,1:T(8,128)S(1)} collective-permute-done((f32[384,64]{0,1:T(8,128)S(1)}, f32[384,64]{0,1:T(8,128)S(1)}, u32[]{:S(2)}, u32[]{:S(2)}) %collective-permute-start.10) | collective-permute-done | bytes 98336 | tf_op jit(solution)/shard_map/ppermute | solution.py:18
  114.7 6.1 %collective-permute-done.11 = f32[384,64]{0,1:T(8,128)S(1)} collective-permute-done((f32[384,64]{0,1:T(8,128)S(1)}, f32[384,64]{0,1:T(8,128)S(1)}, u32[]{:S(2)}, u32[]{:S(2)}) %collective-permute-start.11) | collective-permute-done | bytes 98336 | tf_op jit(solution)/shard_map/ppermute | solution.py:18
  121.5 6.1 %collective-permute-done.12 = f32[384,64]{0,1:T(8,128)S(1)} collective-permute-done((f32[384,64]{0,1:T(8,128)S(1)}, f32[384,64]{0,1:T(8,128)S(1)}, u32[]{:S(2)}, u32[]{:S(2)}) %collective-permute-start.12) | collective-permute-done | bytes 98336 | tf_op jit(solution)/shard_map/ppermute | solution.py:18
  128.2 6.1 %collective-permute-done.13 = f32[384,64]{0,1:T(8,128)S(1)} collective-permute-done((f32[384,64]{0,1:T(8,128)S(1)}, f32[384,64]{0,1:T(8,128)S(1)}, u32[]{:S(2)}, u32[]{:S(2)}) %collective-permute-start.13) | collective-permute-done | bytes 98336 | tf_op jit(solution)/shard_map/ppermute | solution.py:18
  135.2 6.1 %collective-permute-done.14 = f32[384,64]{0,1:T(8,128)S(1)} collective-permute-done((f32[384,64]{0,1:T(8,128)S(1)}, f32[384,64]{0,1:T(8,128)S(1)}, u32[]{:S(2)}, u32[]{:S(2)}) %collective-permute-start.14) | collective-permute-done | bytes 98336 | tf_op jit(solution)/shard_map/ppermute | solution.py:18
  141.9 5.7 %fusion.45 = (f32[48,32]{0,1:T(8,128)S(1)}, f32[48,32,384]{2,0,1:T(8,128)S(1)}) fusion(f32[48,384,32]{1,2,0:T(8,128)} %fusion.9, f32[384,32,32]{0,2,1:T(8,128)} %bitcast.71, f32[48,32,32]{0,2,1:T(8,128)S(1)} %bitcast.70), kind=kOutput, calls=%fused_computation.79 | convolution fusion | flops 228260352 | bytes 6494208 | tf_op jit(solution)/shard_map/ihd,jhd->ihj/dot_general | solution.py:52
  148.4 4.3 %fusion.20 = f32[48,32,32]{0,2,1:T(8,128)S(1)} fusion(f32[384,32,32]{0,2,1:T(8,128)} %bitcast, f32[48,32,384]{2,0,1:T(8,128)S(1)} %get-tuple-element.38, f32[48,32]{0,1:T(8,128)S(1)} %get-tuple-element.37), kind=kOutput, calls=%fused_computation.22 | convolution fusion | flops 227082240 | bytes 4134912 | tf_op jit(solution)/shard_map/ihj,jhd->ihd/dot_general | solution.py:56
  152.8 4.8 %all-gather.3 = f32[2,48,32]{1,2,0:T(8,128)S(1)} all-gather(f32[1,48,32]{1,2,0:T(8,128)S(1)} %bitcast.72), channel_id=3, replica_groups=mesh['row'=16,'col'=2] {'col'}, dimensions={0}, use_global_device_ids=true | all-gather | bytes 18432 | tf_op jit(solution)/shard_map/all_gather | solution.py:28
  157.6 4.6 %all-gather.4 = f32[2,48,32]{1,2,0:T(8,128)S(1)} all-gather(f32[1,48,32]{1,2,0:T(8,128)S(1)} %bitcast.73), channel_id=4, replica_groups=mesh['row'=16,'col'=2] {'col'}, dimensions={0}, use_global_device_ids=true | all-gather | bytes 18432 | tf_op jit(solution)/shard_map/all_gather | solution.py:28
  163.2 12.8 %all-gather = f32[96,32,32]{2,1,0:T(8,128)S(1)} all-gather(f32[48,32,32]{2,1,0:T(8,128)S(1)} %copy.51), channel_id=2, replica_groups=mesh['row'=16,'col'=2] {'col'}, dimensions={0}, use_global_device_ids=true | all-gather | bytes 589824 | tf_op jit(solution)/shard_map/all_gather | solution.py:28
  179.5 4.9 %all-reduce.1 = (f32[48]{0:T(128)S(1)}, f32[48]{0:T(128)S(1)}) all-reduce(f32[48]{0:T(128)S(1)} %get-tuple-element.19, f32[48]{0:T(128)S(1)} %get-tuple-element.18), channel_id=1, replica_groups=mesh['row'=16,'col'=2] {'col'}, use_global_device_ids=true, to_apply=%region_7.8 | all-reduce | flops 96 | bytes 768 | tf_op jit(solution)/shard_map/psum | solution.py:84
  185.1 9.1 %all-reduce = (f32[48,64]{1,0:T(8,128)S(1)}, f32[48,64]{1,0:T(8,128)S(1)}) all-reduce(f32[48,64]{1,0:T(8,128)S(1)} %fusion.24, f32[48,64]{1,0:T(8,128)S(1)} %fusion.25), channel_id=1, replica_groups=mesh['row'=16,'col'=2] {'col'}, use_global_device_ids=true, to_apply=%region_9.10 | all-reduce | flops 6144 | bytes 49152 | tf_op jit(solution)/shard_map/psum | solution.py:92
  194.3 18.8 %all_gather.35 = f32[768,64]{1,0:T(8,128)S(1)} all-gather(f32[48,64]{1,0:T(8,128)S(1)} %get-tuple-element.20), channel_id=1, replica_groups=mesh['row'=16,'col'=2] {'row'}, dimensions={0}, use_global_device_ids=true | all-gather | bytes 208896 | tf_op jit(solution)/shard_map/all_gather | solution.py:93
  213.5 22.6 %fusion.46 = (f32[48,384]{0,1:T(8,128)S(1)}, f32[48,384,128]{2,0,1:T(8,128)}) fusion(f32[128]{0:T(128)S(1)} %copy-done.11, f32[384,128]{1,0:T(8,128)S(1)} %fusion.30, f32[48,128]{1,0:T(8,128)S(1)} %fusion.32, f32[64,128]{1,0:T(8,128)S(1)} %slice-done.6, f32[384,64]{1,0:T(8,128)S(1)} %constant_dynamic-slice_fusion, f32[48,64]{1,0:T(8,128)S(1)} %get-tuple-element.21, ...), kind=kOutput, calls=%fused_computation.80 | convolution fusion | flops 1826863104 | bytes 19313152 | tf_op jit(solution)/shard_map/ip,jpc->ijc/dot_general | solution.py:102
  236.3 10.5 %copy.56 = f32[48,384,128]{2,1,0:T(8,128)} copy(f32[48,384,128]{2,0,1:T(8,128)} %get-tuple-element.41) | data formatting | bytes 18874368 | tf_op jit(solution)/shard_map/add | solution.py:107
  246.9 5.4 %multiply_reduce_fusion = f32[48,384]{0,1:T(8,128)S(1)} fusion(f32[48,384,128]{2,0,1:T(8,128)S(1)} %bitcast.65, f32[48,384]{0,1:T(8,128)S(1)} %copy.58), kind=kLoop, calls=%fused_computation.9 | loop fusion | flops 7059456 | bytes 9584640 | tf_op jit(solution)/shard_map/reduce_sum | solution.py:39
  252.5 11.4 %fusion.8 = f32[18432,128]{1,0:T(8,128)S(1)} fusion(f32[48,384,128]{2,1,0:T(8,128)} %copy.56, f32[18432]{0:T(1024)S(1)} %rsqrt.26, f32[18432]{0:T(1024)S(1)} %div.39), kind=kLoop, calls=%fused_computation.7 | loop fusion | flops 4718592 | bytes 19021824 | tf_op jit(solution)/shard_map/mul | solution.py:39
  263.9 33.8 %fusion.47 = f32[18432,512]{1,0:T(8,128)} fusion(f32[18432,128]{1,0:T(8,128)S(1)} %fusion.8, f32[128,512]{1,0:T(8,128)S(1)} %copy-done.4), kind=kOutput, calls=%fused_computation.81 | convolution fusion | flops 14495514624 | bytes 47448064 | tf_op jit(solution)/shard_map/dot_general | solution.py:109
  297.8 35.4 %fusion.2 = f32[18432,128]{1,0:T(8,128)} fusion(f32[18432,128]{1,0:T(8,128)S(1)} %bitcast.68, f32[512,128]{1,0:T(8,128)S(1)} %copy-done.5, f32[18432,512]{1,0:T(8,128)} %fusion.47), kind=kOutput, calls=%fused_computation.2 | convolution fusion | flops 14507311104 | bytes 56885248 | tf_op jit(solution)/shard_map/dot_general | solution.py:110
  (101 shorter events, 20.7 us)
Async XLA Ops:
  7.2 169.9 %copy-start = (f32[1024,512]{1,0:T(8,128)S(1)}, f32[1024,512]{1,0:T(8,128)}, u32[]{:S(2)}) copy-start(f32[1024,512]{1,0:T(8,128)} %param.19) | copy-start | bytes 6291460
  7.2 134.8 %all-gather.7.cloned.1.call-start = ((), (), s32[]{:S(2)}) async-start(), calls=%async_computation | async-start | bytes 1671168 | tf_op jit(solution)/shard_map/all_gather | solution.py:73
  7.9 38.8 %collective-permute-start = (f32[384,64]{0,1:T(8,128)}, f32[384,64]{0,1:T(8,128)S(1)}, u32[]{:S(2)}, u32[]{:S(2)}) collective-permute-start(f32[384,64]{0,1:T(8,128)} %param.16), channel_id=1, source_target_pairs={{0,2},{2,4},{4,6},{6,8},{8,10},{10,12},{12,14},{14,16},{16,18},{18... | collective-permute-start | bytes 294920 | tf_op jit(solution)/shard_map/ppermute | solution.py:18
  28.8 17.2 %copy-start.8 = (f32[384,64]{0,1:T(8,128)S(1)}, f32[384,64]{0,1:T(8,128)}, u32[]{:S(2)}) copy-start(f32[384,64]{0,1:T(8,128)} %param.16) | copy-start | bytes 294916
  46.7 6.7 %collective-permute-start.1 = (f32[384,64]{0,1:T(8,128)S(1)}, f32[384,64]{0,1:T(8,128)S(1)}, u32[]{:S(2)}, u32[]{:S(2)}) collective-permute-start(f32[384,64]{0,1:T(8,128)S(1)} %collective-permute-done), channel_id=1, source_target_pairs={{0,2},{2,4},{4,6},{6,8},{8,10},{10,12},{12,14},{14,16},{16,18},{18... | collective-permute-start | bytes 294920 | tf_op jit(solution)/shard_map/ppermute | solution.py:18
  53.4 6.7 %collective-permute-start.2 = (f32[384,64]{0,1:T(8,128)S(1)}, f32[384,64]{0,1:T(8,128)S(1)}, u32[]{:S(2)}, u32[]{:S(2)}) collective-permute-start(f32[384,64]{0,1:T(8,128)S(1)} %collective-permute-done.1), channel_id=1, source_target_pairs={{0,2},{2,4},{4,6},{6,8},{8,10},{10,12},{12,14},{14,16},{16,18},{18... | collective-permute-start | bytes 294920 | tf_op jit(solution)/shard_map/ppermute | solution.py:18
  60.2 6.7 %collective-permute-start.3 = (f32[384,64]{0,1:T(8,128)S(1)}, f32[384,64]{0,1:T(8,128)S(1)}, u32[]{:S(2)}, u32[]{:S(2)}) collective-permute-start(f32[384,64]{0,1:T(8,128)S(1)} %collective-permute-done.2), channel_id=1, source_target_pairs={{0,2},{2,4},{4,6},{6,8},{8,10},{10,12},{12,14},{14,16},{16,18},{18... | collective-permute-start | bytes 294920 | tf_op jit(solution)/shard_map/ppermute | solution.py:18
  66.9 6.7 %collective-permute-start.4 = (f32[384,64]{0,1:T(8,128)S(1)}, f32[384,64]{0,1:T(8,128)S(1)}, u32[]{:S(2)}, u32[]{:S(2)}) collective-permute-start(f32[384,64]{0,1:T(8,128)S(1)} %collective-permute-done.3), channel_id=1, source_target_pairs={{0,2},{2,4},{4,6},{6,8},{8,10},{10,12},{12,14},{14,16},{16,18},{18... | collective-permute-start | bytes 294920 | tf_op jit(solution)/shard_map/ppermute | solution.py:18
  73.6 6.7 %collective-permute-start.5 = (f32[384,64]{0,1:T(8,128)S(1)}, f32[384,64]{0,1:T(8,128)S(1)}, u32[]{:S(2)}, u32[]{:S(2)}) collective-permute-start(f32[384,64]{0,1:T(8,128)S(1)} %collective-permute-done.4), channel_id=1, source_target_pairs={{0,2},{2,4},{4,6},{6,8},{8,10},{10,12},{12,14},{14,16},{16,18},{18... | collective-permute-start | bytes 294920 | tf_op jit(solution)/shard_map/ppermute | solution.py:18
  80.4 6.7 %collective-permute-start.6 = (f32[384,64]{0,1:T(8,128)S(1)}, f32[384,64]{0,1:T(8,128)S(1)}, u32[]{:S(2)}, u32[]{:S(2)}) collective-permute-start(f32[384,64]{0,1:T(8,128)S(1)} %collective-permute-done.5), channel_id=1, source_target_pairs={{0,2},{2,4},{4,6},{6,8},{8,10},{10,12},{12,14},{14,16},{16,18},{18... | collective-permute-start | bytes 294920 | tf_op jit(solution)/shard_map/ppermute | solution.py:18
  87.1 6.7 %collective-permute-start.7 = (f32[384,64]{0,1:T(8,128)S(1)}, f32[384,64]{0,1:T(8,128)S(1)}, u32[]{:S(2)}, u32[]{:S(2)}) collective-permute-start(f32[384,64]{0,1:T(8,128)S(1)} %collective-permute-done.6), channel_id=1, source_target_pairs={{0,2},{2,4},{4,6},{6,8},{8,10},{10,12},{12,14},{14,16},{16,18},{18... | collective-permute-start | bytes 294920 | tf_op jit(solution)/shard_map/ppermute | solution.py:18
  93.9 6.7 %collective-permute-start.8 = (f32[384,64]{0,1:T(8,128)S(1)}, f32[384,64]{0,1:T(8,128)S(1)}, u32[]{:S(2)}, u32[]{:S(2)}) collective-permute-start(f32[384,64]{0,1:T(8,128)S(1)} %collective-permute-done.7), channel_id=1, source_target_pairs={{0,2},{2,4},{4,6},{6,8},{8,10},{10,12},{12,14},{14,16},{16,18},{18... | collective-permute-start | bytes 294920 | tf_op jit(solution)/shard_map/ppermute | solution.py:18
  100.6 6.7 %collective-permute-start.9 = (f32[384,64]{0,1:T(8,128)S(1)}, f32[384,64]{0,1:T(8,128)S(1)}, u32[]{:S(2)}, u32[]{:S(2)}) collective-permute-start(f32[384,64]{0,1:T(8,128)S(1)} %collective-permute-done.8), channel_id=1, source_target_pairs={{0,2},{2,4},{4,6},{6,8},{8,10},{10,12},{12,14},{14,16},{16,18},{18... | collective-permute-start | bytes 294920 | tf_op jit(solution)/shard_map/ppermute | solution.py:18
  107.3 6.7 %collective-permute-start.10 = (f32[384,64]{0,1:T(8,128)S(1)}, f32[384,64]{0,1:T(8,128)S(1)}, u32[]{:S(2)}, u32[]{:S(2)}) collective-permute-start(f32[384,64]{0,1:T(8,128)S(1)} %collective-permute-done.9), channel_id=1, source_target_pairs={{0,2},{2,4},{4,6},{6,8},{8,10},{10,12},{12,14},{14,16},{16,18},{18... | collective-permute-start | bytes 294920 | tf_op jit(solution)/shard_map/ppermute | solution.py:18
  114.1 6.7 %collective-permute-start.11 = (f32[384,64]{0,1:T(8,128)S(1)}, f32[384,64]{0,1:T(8,128)S(1)}, u32[]{:S(2)}, u32[]{:S(2)}) collective-permute-start(f32[384,64]{0,1:T(8,128)S(1)} %collective-permute-done.10), channel_id=1, source_target_pairs={{0,2},{2,4},{4,6},{6,8},{8,10},{10,12},{12,14},{14,16},{16,18},{18... | collective-permute-start | bytes 294920 | tf_op jit(solution)/shard_map/ppermute | solution.py:18
  120.8 6.7 %collective-permute-start.12 = (f32[384,64]{0,1:T(8,128)S(1)}, f32[384,64]{0,1:T(8,128)S(1)}, u32[]{:S(2)}, u32[]{:S(2)}) collective-permute-start(f32[384,64]{0,1:T(8,128)S(1)} %collective-permute-done.11), channel_id=1, source_target_pairs={{0,2},{2,4},{4,6},{6,8},{8,10},{10,12},{12,14},{14,16},{16,18},{18... | collective-permute-start | bytes 294920 | tf_op jit(solution)/shard_map/ppermute | solution.py:18
  127.6 6.7 %collective-permute-start.13 = (f32[384,64]{0,1:T(8,128)S(1)}, f32[384,64]{0,1:T(8,128)S(1)}, u32[]{:S(2)}, u32[]{:S(2)}) collective-permute-start(f32[384,64]{0,1:T(8,128)S(1)} %collective-permute-done.12), channel_id=1, source_target_pairs={{0,2},{2,4},{4,6},{6,8},{8,10},{10,12},{12,14},{14,16},{16,18},{18... | collective-permute-start | bytes 294920 | tf_op jit(solution)/shard_map/ppermute | solution.py:18
  134.3 7.0 %collective-permute-start.14 = (f32[384,64]{0,1:T(8,128)S(1)}, f32[384,64]{0,1:T(8,128)S(1)}, u32[]{:S(2)}, u32[]{:S(2)}) collective-permute-start(f32[384,64]{0,1:T(8,128)S(1)} %collective-permute-done.13), channel_id=1, source_target_pairs={{0,2},{2,4},{4,6},{6,8},{8,10},{10,12},{12,14},{14,16},{16,18},{18... | collective-permute-start | bytes 294920 | tf_op jit(solution)/shard_map/ppermute | solution.py:18
  175.9 8.5 %copy-start.6 = (f32[512,64]{0,1:T(8,128)S(1)}, f32[512,64]{0,1:T(8,128)}, u32[]{:S(2)}) copy-start(f32[512,64]{0,1:T(8,128)} %param.21) | copy-start | bytes 393220
  176.7 17.5 %copy-start.3 = (f32[128,128]{1,0:T(8,128)S(1)}, f32[128,128]{1,0:T(8,128)}, u32[]{:S(2)}) copy-start(f32[128,128]{1,0:T(8,128)} %param.22) | copy-start | bytes 196612
  177.1 36.4 %slice-start.6 = ((f32[128,128]{1,0:T(8,128)}), f32[64,128]{1,0:T(8,128)S(1)}, s32[]{:S(2)}) async-start(f32[128,128]{1,0:T(8,128)} %param.22), calls=%async_computation.7 | async-start | bytes 65536 | tf_op jit(solution)/shard_map/slice | solution.py:96
  177.1 36.3 %copy-start.11 = (f32[128]{0:T(128)S(1)}, f32[128]{0:T(128)}, u32[]{:S(2)}) copy-start(f32[128]{0:T(128)} %param.23) | copy-start | bytes 1540
  179.5 56.6 %copy-start.2 = (f32[48,512]{1,0:T(8,128)}, f32[48,512]{1,0:T(8,128)S(1)}, u32[]{:S(2)}) copy-start(f32[48,512]{1,0:T(8,128)S(1)} %get-tuple-element.39) | copy-start | bytes 294916
  236.2 10.7 %slice-start = ((s8[9437184]{0:T(1024)(128)(4,1)}), s8[1048576]{0:T(1024)(128)(4,1)S(1)}, s32[]{:S(2)}) async-start(s8[9437184]{0:T(1024)(128)(4,1)} %bitcast.64), calls=%async_computation.1 | async-start | bytes 2097152
  236.3 10.5 %slice-start.1 = ((s8[9437184]{0:T(1024)(128)(4,1)}), s8[4194304]{0:T(1024)(128)(4,1)S(1)}, s32[]{:S(2)}) async-start(s8[9437184]{0:T(1024)(128)(4,1)} %bitcast.64), calls=%async_computation.2 | async-start | bytes 8388608
  236.3 10.5 %slice-start.2 = ((s8[9437184]{0:T(1024)(128)(4,1)}), s8[4194304]{0:T(1024)(128)(4,1)S(1)}, s32[]{:S(2)}) async-start(s8[9437184]{0:T(1024)(128)(4,1)} %bitcast.64), calls=%async_computation.3 | async-start | bytes 8388608
  252.5 11.4 %copy-start.4 = (f32[128,512]{1,0:T(8,128)S(1)}, f32[128,512]{1,0:T(8,128)}, u32[]{:S(2)}) copy-start(f32[128,512]{1,0:T(8,128)} %param.24) | copy-start | bytes 786436
  252.5 45.3 %slice-start.3 = ((s8[9437184]{0:T(1024)(128)(4,1)}), s8[4194304]{0:T(1024)(128)(4,1)S(1)}, s32[]{:S(2)}) async-start(s8[9437184]{0:T(1024)(128)(4,1)} %bitcast.66), calls=%async_computation.4 | async-start | bytes 8388608
  263.9 33.9 %slice-start.4 = ((s8[9437184]{0:T(1024)(128)(4,1)}), s8[4194304]{0:T(1024)(128)(4,1)S(1)}, s32[]{:S(2)}) async-start(s8[9437184]{0:T(1024)(128)(4,1)} %bitcast.66), calls=%async_computation.5 | async-start | bytes 8388608
  263.9 33.8 %slice-start.5 = ((s8[9437184]{0:T(1024)(128)(4,1)}), s8[1048576]{0:T(1024)(128)(4,1)S(1)}, s32[]{:S(2)}) async-start(s8[9437184]{0:T(1024)(128)(4,1)} %bitcast.66), calls=%async_computation.6 | async-start | bytes 2097152
  263.9 33.8 %copy-start.5 = (f32[512,128]{1,0:T(8,128)S(1)}, f32[512,128]{1,0:T(8,128)}, u32[]{:S(2)}) copy-start(f32[512,128]{1,0:T(8,128)} %param.25) | copy-start | bytes 786436
  297.8 35.5 %copy-start.1 = (f32[1024,512]{1,0:T(8,128)S(1)}, f32[1024,512]{1,0:T(8,128)}, u32[]{:S(2)}) copy-start(f32[1024,512]{1,0:T(8,128)} %param.19) | copy-start | bytes 6291460
  (3 other events, 21.8 us)
Sparse Core Ops, SparseCore 0:
  10.3 42.3 all-gather.6
